TPU v7x, 32 devices: a whole 2x2x4 slice. The times are simulated.
32 devices in a mesh: cent: 8 (over y, x, core), rep: 4 (over z).
Axes of the slice: x: 2, y: 2, z: 4, core: 2. Of those that a mesh axis runs over, the one named last changes fastest.
Arguments:
- points: bfloat16 [16384, 1024], P(('cent', 'rep')), may hold values from -6 to 6
- centroids: bfloat16 [4096, 1024], P('cent'), may hold values from -6 to 6
- owners: int32 [16384, 2], P(('cent', 'rep')), may hold values from 0 to 7, all different within a row; in each aligned block of 512 rows (0 to 511, 512 to 1023, ...) at most 320 rows name the same one
- blocks: int32 [16384, 2, 4], P(('cent', 'rep')), may hold values from 0 to 7, all different within a row
- duals: float32 [4096], P('cent'), may hold values from -1 to 1
Outputs:
- new_centroids: bfloat16 [4096, 1024], P('cent')
- duals_out: float32 [4096], P('cent')
Inputs may be any that keep to these rules, and one draw needn't show every extreme that they name: `owners`: each point names 2 different owner shards; among the points of one device no shard is named more than 320 times, a bound that some block reaches. `blocks`: the 4 block numbers that a point names within one owner shard differ.
All inputs are finite; a program needn't handle non-finite values.
Results may differ from a plain program's by a relative error of at most 0.012.
The roundings to bfloat16 on the way count: a program that leaves them out, or rounds other values in their place, can miss the bound.
Values may be sent and summed in bfloat16 or wider, within the bound.
A program may use at most 64 MiB of HBM per device.

v0:
```python
import functools

import jax
import jax.numpy as jnp
from jax import lax
from jax.experimental import pallas as pl
from jax.experimental.pallas import tpu as pltpu
from jax.sharding import PartitionSpec as P

BLOCKS_DEV = 8
CAND = 4
SINK = 3
ITERS = 2
LANES = 128
SUBLANES = 8
OUT_PIECES = 4
MESH = pl.DeviceIdType.MESH
VMEM_LIMIT = 64000000


softness_factor = 0.02
EPSILON = 1e-06


def normalize(values):
    widened = values.astype(jnp.float32)
    return (
        widened * lax.rsqrt(jnp.mean(widened * widened, axis=-1, keepdims=True) + EPSILON)
    ).astype(jnp.bfloat16)


def candidate_mask(labels_in, block_span):
    member = jnp.any(
        labels_in[:, :, None] == jnp.arange(BLOCKS_DEV, dtype=jnp.int32)[None, None, :], axis=1
    )
    return jnp.repeat(member.astype(jnp.float32), block_span, axis=1)


def kernel_of(slot_rows, slot_mask, centroid_unit, feature_dimension):
    affinity_scores = lax.dot_general(
        slot_rows, centroid_unit, (((1,), (1,)), ((), ())), preferred_element_type=jnp.float32
    ) / (feature_dimension * softness_factor)
    return jnp.exp(affinity_scores) * slot_mask


def routed_body(points, centroids, owners, blocks, duals):
    point_rows, feature_dimension = points.shape
    shard_rows = centroids.shape[0]
    shards = lax.axis_size("cent")
    replicas = lax.axis_size("rep")
    routes = owners.shape[1]
    capacity = 5 * point_rows // shards
    block_span = shard_rows // BLOCKS_DEV
    target = point_rows * replicas / shard_rows
    unit_rows = normalize(points)
    flat_owner = owners.reshape(-1)
    flat_point = jnp.arange(point_rows * routes, dtype=jnp.int32) // routes
    onehot = (flat_owner[:, None] == jnp.arange(shards, dtype=jnp.int32)[None, :]).astype(jnp.int32)
    position = jnp.sum((jnp.cumsum(onehot, axis=0) - onehot) * onehot, axis=1)
    outgoing = (
        jnp.zeros((shards, capacity, feature_dimension), jnp.bfloat16)
        .at[flat_owner, position]
        .set(unit_rows[flat_point])
    )
    labels = (
        jnp.full((shards, capacity, CAND), -1, jnp.int32)
        .at[flat_owner, position]
        .set(blocks.reshape(-1, CAND))
    )
    first_unit = normalize(centroids)
    received_rows = (
        lax.all_to_all(outgoing, "cent", split_axis=0, concat_axis=0, tiled=True),
        lax.all_to_all(labels, "cent", split_axis=0, concat_axis=0, tiled=True),
    )
    slot_rows = received_rows[0].reshape(-1, feature_dimension)
    slot_mask = candidate_mask(received_rows[1].reshape(-1, CAND), block_span)
    first_kernel = kernel_of(slot_rows, slot_mask, first_unit, feature_dimension)
    current = centroids
    duals_now = duals
    for loop_counter in range(ITERS):
        if loop_counter == 0:
            kernel = first_kernel
        else:
            kernel = kernel_of(slot_rows, slot_mask, normalize(current), feature_dimension)
        for turn_index in range(SINK + 1):
            scaling = jnp.exp(duals_now)
            partial_rows = jnp.dot(kernel, scaling, precision=lax.Precision.HIGHEST).reshape(
                shards, capacity
            )
            returned = lax.all_to_all(partial_rows, "cent", split_axis=0, concat_axis=0, tiled=True)
            totals = jnp.sum(returned[flat_owner, position].reshape(point_rows, routes), axis=1)
            inverse = 1.0 / totals
            spread = (
                jnp.zeros((shards, capacity), jnp.float32)
                .at[flat_owner, position]
                .set(inverse[flat_point])
            )
            row_scale = lax.all_to_all(
                spread, "cent", split_axis=0, concat_axis=0, tiled=True
            ).reshape(-1)
            if turn_index < SINK:
                local_mass = jnp.dot(row_scale, kernel, precision=lax.Precision.HIGHEST) * scaling
                column_mass = lax.psum(local_mass, "rep")
                duals_now = duals_now + jnp.log(2.0 * target) - jnp.log(column_mass + target)
        weights = (row_scale[:, None] * kernel * scaling[None, :]).astype(jnp.bfloat16)
        share_sums = lax.psum_scatter(
            lax.dot_general(
                weights, slot_rows, (((0,), (0,)), ((), ())), preferred_element_type=jnp.float32
            ),
            "rep",
            scatter_dimension=0,
            tiled=True,
        )
        current = lax.all_gather(normalize(share_sums), "rep", axis=0, tiled=True)
    return (current, duals_now)


def fused_kernel(
    dims,
    points_ref,
    centroids_ref,
    mask_ref,
    duals_ref,
    out_ref,
    duals_out_ref,
    units,
    masks,
    kern,
    cunit,
    scale_cols,
    mass_cols,
    sums,
    row_parts,
    col_parts,
    sums_out,
    sums_in,
    unit_send,
    unit_recv,
    mask_send,
    mask_recv,
    row_send,
    row_recv,
    col_send,
    col_recv,
    sum_send,
    sum_recv,
    new_send,
    new_recv,
):
    shards, replicas, point_rows, shard_rows, features = dims
    span = shard_rows // BLOCKS_DEV
    pieces = 4
    piece = point_rows // pieces
    dual_rows = shard_rows // LANES
    groups_out = OUT_PIECES
    group = shard_rows // groups_out
    cut = group // replicas
    target = point_rows * replicas / shard_rows
    inverse_soft = 1.0 / (features * softness_factor)

    me = lax.axis_index("cent")
    z = lax.axis_index("rep")
    core = me % 2
    xpos = (me // 2) % 2
    ypos = me // 4

    def rel(direction):
        dc, dx, dy = direction % 2, (direction // 2) % 2, direction // 4
        c = 1 - core if dc else core
        x = 1 - xpos if dx else xpos
        y = 1 - ypos if dy else ypos
        return (y * 2 + x) * 2 + c

    peer = [rel(d) for d in range(shards)]
    zpeer = [(z + k) % replicas for k in range(replicas)]

    at_end = jnp.logical_or(z == 0, z == replicas - 1)
    in_mid = jnp.logical_not(at_end)
    partner = z + 1 - 2 * (z % 2)
    low = z // 2
    far_end = 3 - 3 * low
    far_mid = 2 - low

    barrier = pltpu.get_barrier_semaphore()
    for d in range(1, shards):
        pl.semaphore_signal(barrier, inc=1, device_id=(peer[d], z), device_id_type=MESH)
    for k in range(1, replicas):
        pl.semaphore_signal(barrier, inc=1, device_id=(me, zpeer[k]), device_id_type=MESH)
    pl.semaphore_wait(barrier, shards - 1 + replicas - 1)

    mask_copies = []
    for d in range(1, shards):
        copy = pltpu.make_async_remote_copy(
            src_ref=mask_ref.at[peer[d]],
            dst_ref=masks.at[d],
            send_sem=mask_send.at[d],
            recv_sem=mask_recv.at[d],
            device_id=(peer[d], z),
            device_id_type=MESH,
        )
        copy.start()
        mask_copies.append(copy)
    masks[0] = mask_ref[me]

    unit_copies = {}

    def push(slot, chunk, direction):
        rows = pl.ds(chunk * piece, piece)
        copy = pltpu.make_async_remote_copy(
            src_ref=units.at[slot, rows],
            dst_ref=units.at[slot ^ direction, rows],
            send_sem=unit_send.at[slot, chunk, direction // 2],
            recv_sem=unit_recv.at[slot ^ direction, chunk],
            device_id=(peer[direction], z),
            device_id_type=MESH,
        )
        copy.start()
        unit_copies[(slot, chunk, direction)] = copy

    def arrive(slot, chunk):
        rows = pl.ds(chunk * piece, piece)
        pltpu.make_async_copy(
            units.at[slot, rows], units.at[slot, rows], unit_recv.at[slot, chunk]
        ).wait()

    order_x = (0, 1, 2, 3)
    order_y = (2, 3, 0, 1)
    for step in (0, 2, 1, 3):
        rows = pl.ds(step * piece, piece)
        units[0, rows] = normalize(points_ref[rows])
        if step == 0:
            push(0, 0, 2)
        if step == 2:
            push(0, 2, 4)
        if step == 1:
            push(0, 1, 2)
            push(0, 2, 2)
        if step == 3:
            push(0, 3, 4)
            push(0, 3, 2)
            push(0, 0, 4)
            push(0, 1, 4)
    for step in range(pieces):
        push(0, step, 1)

    cunit[...] = normalize(centroids_ref[...])

    def block_kernel(slot, start=0, count=shard_rows, first=0, width=point_rows):
        held = pl.ds(first, width)
        scores = lax.dot_general(
            cunit[pl.ds(start, count), :],
            units[slot, held, :],
            (((1,), (1,)), ((), ())),
            preferred_element_type=jnp.float32,
        )
        marks = masks[slot, :, held]
        for b in range(count // span):
            rows = pl.ds(start + b * span, span)
            mark = marks[start // span + b : start // span + b + 1, :]
            kern[slot, rows, held] = (
                jnp.exp(scores[b * span : (b + 1) * span] * inverse_soft) * mark
            )

    def half_kernels(halves):
        for slot, chunks in halves:
            block_kernel(slot, first=min(chunks) * piece, width=2 * piece)

    block_kernel(0)
    for step in range(pieces):
        tx, ty = order_x[step], order_y[step]
        arrive(2, tx)
        if step < 2:
            push(2, tx, 4)
        push(2, tx, 1)
        arrive(4, ty)
        if step < 2:
            push(4, ty, 2)
        push(4, ty, 1)
        if step == 1:
            for copy in mask_copies:
                copy.wait()
            for chunk in range(pieces):
                arrive(1, chunk)
            block_kernel(1)
        if step >= 2:
            arrive(6, order_x[step - 2])
            push(6, order_x[step - 2], 1)
            arrive(6, order_y[step - 2])
            push(6, order_y[step - 2], 1)
        if step == 2:
            for slot, chunks in ((3, order_x[:2]), (5, order_y[:2])):
                for chunk in chunks:
                    arrive(slot, chunk)
            half_kernels(((2, order_x[:2]), (4, order_y[:2]), (3, order_x[:2]), (5, order_y[:2])))
    half_kernels(((2, order_x[2:]), (4, order_y[2:])))
    for slot, chunks in ((3, order_x[2:]), (5, order_y[2:])):
        for chunk in chunks:
            arrive(slot, chunk)
        half_kernels(((slot, chunks),))
    half_kernels(((6, order_x[:2]), (6, order_y[:2])))
    for chunk in range(pieces):
        arrive(7, chunk)
    half_kernels(((7, order_x[:2]), (7, order_y[:2])))
    for copy in unit_copies.values():
        copy.wait_send()

    duals_now = jnp.concatenate([duals_ref[...]] * (SUBLANES // dual_rows), axis=0)
    groups = shard_rows // SUBLANES
    tiles = point_rows // LANES

    def spread_scale(scaling):
        for t in range(dual_rows):
            row = jnp.broadcast_to(scaling[t : t + 1, :], (LANES, LANES))
            scale_cols[pl.ds(t * LANES, LANES), :] = row.T

    def row_pass():
        def step(g, acc):
            rows = pl.ds(pl.multiple_of(g * SUBLANES, SUBLANES), SUBLANES)
            wide = jnp.concatenate([scale_cols[rows, :]] * tiles, axis=1)
            return tuple(acc[p] + kern[p, rows, :] * wide for p in range(shards))

        zero = jnp.zeros((SUBLANES, point_rows), jnp.float32)
        acc = lax.fori_loop(0, groups, step, (zero,) * shards, unroll=2)
        return jnp.concatenate([jnp.sum(a, axis=0, keepdims=True) for a in acc], axis=0)

    def col_pass(inverse):
        wide = [
            jnp.broadcast_to(inverse[p : p + 1, :], (SUBLANES, point_rows)) for p in range(shards)
        ]

        def step(g, carry):
            rows = pl.ds(pl.multiple_of(g * SUBLANES, SUBLANES), SUBLANES)
            total = kern[0, rows, :] * wide[0]
            for p in range(1, shards):
                total = total + kern[p, rows, :] * wide[p]
            narrow = total[:, :LANES]
            for t in range(1, tiles):
                narrow = narrow + total[:, t * LANES : (t + 1) * LANES]
            mass_cols[rows, :] = narrow
            return carry

        lax.fori_loop(0, groups, step, 0, unroll=2)
        parts = [
            jnp.sum(mass_cols[pl.ds(t * LANES, LANES), :].T, axis=0, keepdims=True)
            for t in range(dual_rows)
        ]
        return jnp.concatenate(parts * (SUBLANES // dual_rows), axis=0)

    def row_exchange(turn, part):
        row_parts[turn, 0] = part
        copies = []
        for d in (6, 7, 2, 4, 3, 5, 1):
            copy = pltpu.make_async_remote_copy(
                src_ref=row_parts.at[turn, 0],
                dst_ref=row_parts.at[turn, d],
                send_sem=row_send.at[turn, d],
                recv_sem=row_recv.at[turn, d],
                device_id=(peer[d], z),
                device_id_type=MESH,
            )
            copy.start()
            copies.append(copy)
        for copy in copies:
            copy.wait()
        rows = []
        for p in range(shards):
            total = part[p : p + 1, :]
            for d in range(1, shards):
                total = total + row_parts[turn, d, pl.ds(p ^ d, 1), :]
            rows.append(total)
        return jnp.concatenate(rows, axis=0)

    def col_exchange(turn, part):
        col_parts[turn, z] = part
        copies = []
        for k in range(1, replicas):
            copy = pltpu.make_async_remote_copy(
                src_ref=col_parts.at[turn, z],
                dst_ref=col_parts.at[turn, z],
                send_sem=col_send.at[turn, k],
                recv_sem=col_recv.at[turn, k],
                device_id=(me, zpeer[k]),
                device_id_type=MESH,
            )
            copy.start()
            copies.append(copy)
        for copy in copies:
            copy.wait()
        total = col_parts[turn, 0]
        for k in range(1, replicas):
            total = total + col_parts[turn, k]
        return total

    row_turn = 0
    col_turn = 0
    for loop_counter in range(ITERS):
        last = loop_counter == ITERS - 1
        for turn_index in range(SINK + 1):
            scaling = jnp.exp(duals_now)
            spread_scale(scaling)
            inverse = 1.0 / row_exchange(row_turn, row_pass())
            row_turn += 1
            if turn_index < SINK:
                mass = col_exchange(col_turn, col_pass(inverse) * scaling)
                col_turn += 1
                duals_now = duals_now + jnp.log(2.0 * target) - jnp.log(mass + target)

        row_parts[row_turn - 1, 0] = inverse

        dest = out_ref if last else cunit

        def part_rows(i, q):
            start = i * group + q * cut
            if not isinstance(q, int):
                start = pl.multiple_of(start, cut)
            return pl.ds(start, cut)

        def sum_copy(i, source, landing, to):
            return pltpu.make_async_remote_copy(
                src_ref=sums_out.at[loop_counter, i, source],
                dst_ref=sums_in.at[loop_counter, i, landing],
                send_sem=sum_send.at[loop_counter, i, source],
                recv_sem=sum_recv.at[loop_counter, i, landing],
                device_id=(me, to),
                device_id_type=MESH,
            )

        def sum_arrive(i, landing):
            ref = sums_in.at[loop_counter, i, landing]
            pltpu.make_async_copy(ref, ref, sum_recv.at[loop_counter, i, landing]).wait()
            return sums_in[loop_counter, i, landing].astype(jnp.float32)

        def new_copy(i, q, to, number):
            return pltpu.make_async_remote_copy(
                src_ref=dest.at[part_rows(i, q)],
                dst_ref=dest.at[part_rows(i, q)],
                send_sem=new_send.at[loop_counter, i, number],
                recv_sem=new_recv.at[loop_counter, i, q],
                device_id=(me, to),
                device_id_type=MESH,
            )

        def new_arrive(i, q):
            ref = dest.at[part_rows(i, q)]
            pltpu.make_async_copy(ref, ref, new_recv.at[loop_counter, i, q]).wait()

        def accumulate(i):
            rows = pl.ds(i * group, group)
            wide = jnp.concatenate([scale_cols[rows, :]] * tiles, axis=1)

            def step(slot, acc):
                inv = row_parts[row_turn - 1, 0, pl.ds(slot, 1), :]
                weights = (inv * kern[slot, rows, :] * wide).astype(jnp.bfloat16)
                return acc + jnp.dot(weights, units[slot], preferred_element_type=jnp.float32)

            zero = jnp.zeros((group, features), jnp.float32)
            sums[rows, :] = lax.fori_loop(0, shards, step, zero)

            def raw(source, q):
                sums_out[loop_counter, i, source] = sums[part_rows(i, q), :].astype(jnp.bfloat16)
                sum_copy(i, source, source, partner).start()

            @pl.when(at_end)
            def _():
                raw(2, far_end)
                raw(3, far_mid)

            raw(0, partner)

        def pair_sums(i):
            @pl.when(in_mid)
            def _():
                for source, q in ((2, far_end), (3, far_mid)):
                    total = sum_arrive(i, source) + sums[part_rows(i, q), :]
                    sums_out[loop_counter, i, source] = total.astype(jnp.bfloat16)
                    sum_copy(i, source, 1, q).start()

        def finish_sums(i):
            mine = part_rows(i, z)
            total = sums[mine, :] + sum_arrive(i, 0)
            fresh = normalize(total + sum_arrive(i, 1))
            dest[mine, :] = fresh if last else normalize(fresh)
            new_copy(i, z, far_mid, 1).start()
            new_copy(i, z, partner, 0).start()

        def forward_new(i):
            @pl.when(in_mid)
            def _():
                for number, q in ((3, far_mid), (2, far_end)):
                    new_arrive(i, q)
                    new_copy(i, q, partner, number).start()

            new_arrive(i, partner)

        def end_new(i):
            @pl.when(at_end)
            def _():
                new_arrive(i, far_mid)
                new_arrive(i, far_end)

        def remake(i):
            if last:
                return

            def step(slot, carry):
                block_kernel(slot, i * group, group)
                return carry

            lax.fori_loop(0, shards, step, 0)

        stages = (accumulate, pair_sums, finish_sums, forward_new, end_new, remake)
        lags = (0, 1, 2, 3, 4, 4)
        for step in range(groups_out + lags[-1]):
            for lag, stage in zip(lags, stages):
                if 0 <= step - lag < groups_out:
                    stage(step - lag)
        for i in range(groups_out):
            for source in (0, 2, 3):
                sum_copy(i, source, source, partner).wait_send()
            new_copy(i, z, partner, 0).wait_send()
            new_copy(i, z, far_mid, 1).wait_send()

            @pl.when(in_mid)
            def _():
                new_copy(i, far_end, partner, 2).wait_send()
                new_copy(i, far_mid, partner, 3).wait_send()

    duals_out_ref[...] = duals_now[:dual_rows]


def fused_body(points, centroids, owners, blocks, duals):
    point_rows, features = points.shape
    shard_rows = centroids.shape[0]
    shards = lax.axis_size("cent")
    replicas = lax.axis_size("rep")
    dims = (shards, replicas, point_rows, shard_rows, features)
    dual_rows = shard_rows // LANES
    cut = shard_rows // (OUT_PIECES * replicas)
    wanted = owners.T[None, None, :, None, :] == jnp.arange(shards, dtype=jnp.int32).reshape(
        -1, 1, 1, 1, 1
    )
    named = jnp.transpose(blocks, (1, 2, 0))[None, None] == jnp.arange(
        BLOCKS_DEV, dtype=jnp.int32
    ).reshape(1, -1, 1, 1, 1)
    mask = jnp.any(jnp.logical_and(wanted, named), axis=(2, 3)).astype(jnp.float32)
    dual_tile = duals.reshape(dual_rows, LANES)
    vmem = pl.BlockSpec(memory_space=pltpu.VMEM)
    row_turns = ITERS * (SINK + 1)
    col_turns = ITERS * SINK
    dma = pltpu.SemaphoreType.DMA
    new_centroids, duals_out = pl.pallas_call(
        functools.partial(fused_kernel, dims),
        out_shape=(
            jax.ShapeDtypeStruct((shard_rows, features), jnp.bfloat16),
            jax.ShapeDtypeStruct((dual_rows, LANES), jnp.float32),
        ),
        in_specs=[vmem] * 4,
        out_specs=(vmem, vmem),
        scratch_shapes=[
            pltpu.VMEM((shards, point_rows, features), jnp.bfloat16),
            pltpu.VMEM((shards, BLOCKS_DEV, point_rows), jnp.float32),
            pltpu.VMEM((shards, shard_rows, point_rows), jnp.float32),
            pltpu.VMEM((shard_rows, features), jnp.bfloat16),
            pltpu.VMEM((shard_rows, LANES), jnp.float32),
            pltpu.VMEM((shard_rows, LANES), jnp.float32),
            pltpu.VMEM((shard_rows, features), jnp.float32),
            pltpu.VMEM((row_turns, shards, shards, point_rows), jnp.float32),
            pltpu.VMEM((col_turns, replicas, SUBLANES, LANES), jnp.float32),
            pltpu.VMEM((ITERS, OUT_PIECES, 4, cut, features), jnp.bfloat16),
            pltpu.VMEM((ITERS, OUT_PIECES, 4, cut, features), jnp.bfloat16),
            dma((shards, 4, 3)),
            dma((shards, 4)),
            dma((shards,)),
            dma((shards,)),
            dma((row_turns, shards)),
            dma((row_turns, shards)),
            dma((col_turns, replicas)),
            dma((col_turns, replicas)),
            dma((ITERS, OUT_PIECES, 4)),
            dma((ITERS, OUT_PIECES, 4)),
            dma((ITERS, OUT_PIECES, 4)),
            dma((ITERS, OUT_PIECES, 4)),
        ],
        compiler_params=pltpu.CompilerParams(
            collective_id=0, has_side_effects=True, vmem_limit_bytes=VMEM_LIMIT
        ),
        name="fused_kmeans",
    )(points, centroids, mask, dual_tile)
    return new_centroids, duals_out.reshape(shard_rows)


def solution(mesh):
    shards = mesh.shape["cent"]

    def body(points, centroids, owners, blocks, duals):
        point_rows, features = points.shape
        shard_rows = centroids.shape[0]
        plane_bytes = shards * point_rows * (2 * features + 4 * shard_rows)
        cube = shards == 2**3 and mesh.shape["rep"] == 2 * 2 and shard_rows % LANES == 0 and SUBLANES % (shard_rows // LANES) == 0
        if cube and plane_bytes <= VMEM_LIMIT // 3:
            return fused_body(points, centroids, owners, blocks, duals)
        return routed_body(points, centroids, owners, blocks, duals)

    return jax.shard_map(
        body,
        mesh=mesh,
        in_specs=(
            P(("cent", "rep"), None),
            P("cent", None),
            P(("cent", "rep"), None),
            P(("cent", "rep"), None, None),
            P("cent"),
        ),
        out_specs=(P("cent", None), P("cent")),
        check_vma=False,
    )
```

profile of v0, /device:TPU:0, one launch (start us, length us, event | category | flops | bytes accessed | tf_op | source)
XLA Modules:
  0.0 203.2 jit_solution(13536036658658766616)
XLA Ops:
  0.6 0.0 copy-start
  0.6 0.7 iota_compare_fusion.1
  1.4 0.0 copy-done
  1.4 0.1 and_reduce_fusion
  1.5 0.7 convert_element_type.3.mask_ref
  2.2 198.2 %fused_kmeans.1 = (bf16[512,1024]{1,0:T(8,128)(2,1)}, f32[4,128]{1,0:T(4,128)}) custom-call(bf16[512,1024]{1,0:T(8,128)(2,1)} %points_ref.1, bf16[512,1024]{1,0:T(8,128)(2,1)} %centroids_ref.1, f32[8,8,512]{2,1,0:T(8,128)} %convert_element_type.3.mask_ref, f32[4,128]{1,0:T(4,128)} %bitcast.6), custom_call_target="tpu_custom_call" | custom-call | tf_op jit(solution)/shard_map/fused_kmeans/pallas_call | solution.py:551
  200.3 0.0 copy-start.1
  200.3 2.3 %copy.9 = bf16[512,1024]{1,0:T(8,128)(2,1)} copy(bf16[512,1024]{1,0:T(8,128)(2,1)} %get-tuple-element.8) | data formatting | bytes 2097152
  202.6 0.0 copy-done.1
  202.6 0.6 copy.10
  (1 shorter events, 0.0 us)
Async XLA Ops:
  0.6 0.7 copy-start
  200.3 2.3 %copy-start.1 = (f32[4,128]{1,0:T(4,128)S(1)}, f32[4,128]{1,0:T(4,128)}, u32[]{:S(2)}) copy-start(f32[4,128]{1,0:T(4,128)} %get-tuple-element.5) | copy-start | bytes 6148
where the time goes:
time: 203 us
  Pallas kernels  198 us (98%)
  local copies, waits for them, and re-layouts  2.85 us (1%)
    pallas_call x1, Pallas kernels, fused_body(): pl.pallas_call(functools.partial(fused_kernel, dims), out_shape=(jax.Shap...  198 us

commit v1 on v0

v1 whole, which is shorter than its diff:
```python
import functools

import jax
import jax.numpy as jnp
from jax import lax
from jax.experimental import pallas as pl
from jax.experimental.pallas import tpu as pltpu
from jax.sharding import PartitionSpec as P

BLOCKS_DEV = 8
CAND = 4
SINK = 3
ITERS = 2
LANES = 128
SUBLANES = 8
SUM_BLOCKS = 4
GROUP_PARTS = (1, 1, 2, 2, 2, 2, 2, 2, 1, 1)
MESH = pl.DeviceIdType.MESH
VMEM_LIMIT = 64000000


softness_factor = 0.02
EPSILON = 1e-06


def normalize(values):
    widened = values.astype(jnp.float32)
    return (
        widened * lax.rsqrt(jnp.mean(widened * widened, axis=-1, keepdims=True) + EPSILON)
    ).astype(jnp.bfloat16)


def candidate_mask(labels_in, block_span):
    member = jnp.any(
        labels_in[:, :, None] == jnp.arange(BLOCKS_DEV, dtype=jnp.int32)[None, None, :], axis=1
    )
    return jnp.repeat(member.astype(jnp.float32), block_span, axis=1)


def kernel_of(slot_rows, slot_mask, centroid_unit, feature_dimension):
    affinity_scores = lax.dot_general(
        slot_rows, centroid_unit, (((1,), (1,)), ((), ())), preferred_element_type=jnp.float32
    ) / (feature_dimension * softness_factor)
    return jnp.exp(affinity_scores) * slot_mask


def routed_body(points, centroids, owners, blocks, duals):
    point_rows, feature_dimension = points.shape
    shard_rows = centroids.shape[0]
    shards = lax.axis_size("cent")
    replicas = lax.axis_size("rep")
    routes = owners.shape[1]
    capacity = 5 * point_rows // shards
    block_span = shard_rows // BLOCKS_DEV
    target = point_rows * replicas / shard_rows
    unit_rows = normalize(points)
    flat_owner = owners.reshape(-1)
    flat_point = jnp.arange(point_rows * routes, dtype=jnp.int32) // routes
    onehot = (flat_owner[:, None] == jnp.arange(shards, dtype=jnp.int32)[None, :]).astype(jnp.int32)
    position = jnp.sum((jnp.cumsum(onehot, axis=0) - onehot) * onehot, axis=1)
    outgoing = (
        jnp.zeros((shards, capacity, feature_dimension), jnp.bfloat16)
        .at[flat_owner, position]
        .set(unit_rows[flat_point])
    )
    labels = (
        jnp.full((shards, capacity, CAND), -1, jnp.int32)
        .at[flat_owner, position]
        .set(blocks.reshape(-1, CAND))
    )
    first_unit = normalize(centroids)
    received_rows = (
        lax.all_to_all(outgoing, "cent", split_axis=0, concat_axis=0, tiled=True),
        lax.all_to_all(labels, "cent", split_axis=0, concat_axis=0, tiled=True),
    )
    slot_rows = received_rows[0].reshape(-1, feature_dimension)
    slot_mask = candidate_mask(received_rows[1].reshape(-1, CAND), block_span)
    first_kernel = kernel_of(slot_rows, slot_mask, first_unit, feature_dimension)
    current = centroids
    duals_now = duals
    for loop_counter in range(ITERS):
        if loop_counter == 0:
            kernel = first_kernel
        else:
            kernel = kernel_of(slot_rows, slot_mask, normalize(current), feature_dimension)
        for turn_index in range(SINK + 1):
            scaling = jnp.exp(duals_now)
            partial_rows = jnp.dot(kernel, scaling, precision=lax.Precision.HIGHEST).reshape(
                shards, capacity
            )
            returned = lax.all_to_all(partial_rows, "cent", split_axis=0, concat_axis=0, tiled=True)
            totals = jnp.sum(returned[flat_owner, position].reshape(point_rows, routes), axis=1)
            inverse = 1.0 / totals
            spread = (
                jnp.zeros((shards, capacity), jnp.float32)
                .at[flat_owner, position]
                .set(inverse[flat_point])
            )
            row_scale = lax.all_to_all(
                spread, "cent", split_axis=0, concat_axis=0, tiled=True
            ).reshape(-1)
            if turn_index < SINK:
                local_mass = jnp.dot(row_scale, kernel, precision=lax.Precision.HIGHEST) * scaling
                column_mass = lax.psum(local_mass, "rep")
                duals_now = duals_now + jnp.log(2.0 * target) - jnp.log(column_mass + target)
        weights = (row_scale[:, None] * kernel * scaling[None, :]).astype(jnp.bfloat16)
        share_sums = lax.psum_scatter(
            lax.dot_general(
                weights, slot_rows, (((0,), (0,)), ((), ())), preferred_element_type=jnp.float32
            ),
            "rep",
            scatter_dimension=0,
            tiled=True,
        )
        current = lax.all_gather(normalize(share_sums), "rep", axis=0, tiled=True)
    return (current, duals_now)


def fused_kernel(
    dims,
    points_ref,
    centroids_ref,
    owners_ref,
    blocks_ref,
    duals_ref,
    out_ref,
    duals_out_ref,
    units,
    marks_out,
    masks,
    kern,
    cunit,
    scale_cols,
    mass_cols,
    weights,
    sums,
    row_parts,
    col_parts,
    raw_out,
    raw_in,
    pair_out,
    pair_in,
    unit_send,
    unit_recv,
    mask_send,
    mask_recv,
    row_send,
    row_recv,
    col_send,
    col_recv,
    raw_send,
    raw_recv,
    pair_send,
    pair_recv,
    new_send,
    new_recv,
):
    shards, replicas, point_rows, shard_rows, features = dims
    span = shard_rows // BLOCKS_DEV
    pieces = 4
    piece = point_rows // pieces
    dual_rows = shard_rows // LANES
    block = shard_rows // SUM_BLOCKS
    group_rows = [shard_rows * part // sum(GROUP_PARTS) for part in GROUP_PARTS]
    starts = [sum(group_rows[:i]) for i in range(len(group_rows))]
    half_rows = shard_rows // 2
    target = point_rows * replicas / shard_rows
    inverse_soft = 1.0 / (features * softness_factor)
    routes = owners_ref.shape[0]

    me = lax.axis_index("cent")
    z = lax.axis_index("rep")
    core = me % 2
    xpos = (me // 2) % 2
    ypos = me // 4

    def rel(direction):
        dc, dx, dy = direction % 2, (direction // 2) % 2, direction // 4
        c = 1 - core if dc else core
        x = 1 - xpos if dx else xpos
        y = 1 - ypos if dy else ypos
        return (y * 2 + x) * 2 + c

    peer = [rel(d) for d in range(shards)]
    zpeer = [(z + k) % replicas for k in range(replicas)]

    at_end = jnp.logical_or(z == 0, z == replicas - 1)
    in_mid = jnp.logical_not(at_end)
    partner = z + 1 - 2 * (z % 2)
    middle = replicas - 1 - z

    barrier = pltpu.get_barrier_semaphore()
    for d in range(1, shards):
        pl.semaphore_signal(barrier, inc=1, device_id=(peer[d], z), device_id_type=MESH)
    for k in range(1, replicas):
        pl.semaphore_signal(barrier, inc=1, device_id=(me, zpeer[k]), device_id_type=MESH)

    def chunk_rows(slot, chunk, count=1):
        start = peer[slot] * point_rows + chunk * piece
        return pl.ds(pl.multiple_of(start, piece), piece * count)

    for step in (0, 2, 1, 3):
        units[chunk_rows(0, step), :] = normalize(points_ref[pl.ds(step * piece, piece), :])

    number = lax.broadcasted_iota(jnp.int32, (BLOCKS_DEV, point_rows), 0)
    named = []
    for r in range(routes):
        hit = blocks_ref[r, 0:1, :] == number
        for c in range(1, CAND):
            hit = jnp.logical_or(hit, blocks_ref[r, c : c + 1, :] == number)
        named.append(hit)
    for s in range(shards):
        marked = jnp.logical_and(owners_ref[0:1, :] == s, named[0])
        for r in range(1, routes):
            marked = jnp.logical_or(marked, jnp.logical_and(owners_ref[r : r + 1, :] == s, named[r]))
        marks_out[s] = jnp.where(marked, 1.0, 0.0)

    pl.semaphore_wait(barrier, shards - 1 + replicas - 1)

    unit_copies = {}

    def push(slot, chunk, direction):
        rows = chunk_rows(slot, chunk)
        copy = pltpu.make_async_remote_copy(
            src_ref=units.at[rows],
            dst_ref=units.at[rows],
            send_sem=unit_send.at[slot, chunk, direction // 2],
            recv_sem=unit_recv.at[slot ^ direction, chunk],
            device_id=(peer[direction], z),
            device_id_type=MESH,
        )
        copy.start()
        unit_copies[(slot, chunk, direction)] = copy

    def arrive(slot, chunk):
        rows = chunk_rows(slot, chunk)
        pltpu.make_async_copy(units.at[rows], units.at[rows], unit_recv.at[slot, chunk]).wait()

    order_x = (0, 1, 2, 3)
    order_y = (2, 3, 0, 1)
    push(0, 0, 2)
    push(0, 2, 4)
    mask_copies = []
    for d in range(1, shards):
        copy = pltpu.make_async_remote_copy(
            src_ref=marks_out.at[peer[d]],
            dst_ref=masks.at[me],
            send_sem=mask_send.at[d],
            recv_sem=mask_recv.at[d],
            device_id=(peer[d], z),
            device_id_type=MESH,
        )
        copy.start()
        mask_copies.append(copy)
    push(0, 1, 2)
    push(0, 3, 4)
    push(0, 2, 2)
    push(0, 0, 4)
    push(0, 3, 2)
    push(0, 1, 4)
    for step in range(pieces):
        push(0, step, 1)
    masks[me] = marks_out[me]

    cunit[...] = normalize(centroids_ref[...])

    def block_kernel(slot, chunk, count):
        held = chunk_rows(slot, chunk, count)
        scores = lax.dot_general(
            cunit[...],
            units[held, :],
            (((1,), (1,)), ((), ())),
            preferred_element_type=jnp.float32,
        )
        marks = masks[peer[slot], :, pl.ds(chunk * piece, count * piece)]
        for b in range(BLOCKS_DEV):
            kern[pl.ds(b * span, span), held] = (
                jnp.exp(scores[b * span : (b + 1) * span] * inverse_soft) * marks[b : b + 1, :]
            )

    def half_kernels(halves):
        for slot, chunks in halves:
            block_kernel(slot, min(chunks), 2)

    half_kernels(((0, (0, 1)), (0, (2, 3))))
    for step in range(pieces):
        tx, ty = order_x[step], order_y[step]
        arrive(2, tx)
        if step < 2:
            push(2, tx, 4)
        push(2, tx, 1)
        arrive(4, ty)
        if step < 2:
            push(4, ty, 2)
        push(4, ty, 1)
        if step == 1:
            for d in range(1, shards):
                pltpu.make_async_copy(
                    masks.at[peer[d]], masks.at[peer[d]], mask_recv.at[d]
                ).wait()
            for chunk in range(pieces):
                arrive(1, chunk)
            half_kernels(((1, (0, 1)), (1, (2, 3))))
        if step >= 2:
            arrive(6, order_x[step - 2])
            push(6, order_x[step - 2], 1)
            arrive(6, order_y[step - 2])
            push(6, order_y[step - 2], 1)
        if step == 2:
            for slot, chunks in ((3, order_x[:2]), (5, order_y[:2])):
                for chunk in chunks:
                    arrive(slot, chunk)
            half_kernels(((2, order_x[:2]), (4, order_y[:2]), (3, order_x[:2]), (5, order_y[:2])))
    half_kernels(((2, order_x[2:]), (4, order_y[2:])))
    for slot, chunks in ((3, order_x[2:]), (5, order_y[2:])):
        for chunk in chunks:
            arrive(slot, chunk)
        half_kernels(((slot, chunks),))
    half_kernels(((6, order_x[:2]), (6, order_y[:2])))
    for chunk in range(pieces):
        arrive(7, chunk)
    half_kernels(((7, order_x[:2]), (7, order_y[:2])))
    for copy in unit_copies.values():
        copy.wait_send()
    for copy in mask_copies:
        copy.wait_send()

    duals_now = jnp.concatenate([duals_ref[...]] * (SUBLANES // dual_rows), axis=0)
    groups = shard_rows // SUBLANES
    tiles = point_rows // LANES

    def slot_columns(p):
        return slice(p * point_rows, (p + 1) * point_rows)

    def spread_scale(scaling):
        for t in range(dual_rows):
            row = jnp.broadcast_to(scaling[t : t + 1, :], (LANES, LANES))
            scale_cols[pl.ds(t * LANES, LANES), :] = row.T

    def row_pass():
        def step(g, acc):
            rows = pl.ds(pl.multiple_of(g * SUBLANES, SUBLANES), SUBLANES)
            wide = jnp.concatenate([scale_cols[rows, :]] * tiles, axis=1)
            return tuple(acc[p] + kern[rows, slot_columns(p)] * wide for p in range(shards))

        zero = jnp.zeros((SUBLANES, point_rows), jnp.float32)
        acc = lax.fori_loop(0, groups, step, (zero,) * shards, unroll=2)
        return jnp.concatenate([jnp.sum(a, axis=0, keepdims=True) for a in acc], axis=0)

    def col_pass(inverse):
        wide = [
            jnp.broadcast_to(inverse[p : p + 1, :], (SUBLANES, point_rows)) for p in range(shards)
        ]

        def step(g, carry):
            rows = pl.ds(pl.multiple_of(g * SUBLANES, SUBLANES), SUBLANES)
            total = kern[rows, slot_columns(0)] * wide[0]
            for p in range(1, shards):
                total = total + kern[rows, slot_columns(p)] * wide[p]
            narrow = total[:, :LANES]
            for t in range(1, tiles):
                narrow = narrow + total[:, t * LANES : (t + 1) * LANES]
            mass_cols[rows, :] = narrow
            return carry

        lax.fori_loop(0, groups, step, 0, unroll=2)
        parts = [
            jnp.sum(mass_cols[pl.ds(t * LANES, LANES), :].T, axis=0, keepdims=True)
            for t in range(dual_rows)
        ]
        return jnp.concatenate(parts * (SUBLANES // dual_rows), axis=0)

    def row_exchange(turn, part):
        row_parts[turn, 0] = part.astype(row_parts.dtype)
        copies = []
        for d in (6, 7, 2, 4, 3, 5, 1):
            copy = pltpu.make_async_remote_copy(
                src_ref=row_parts.at[turn, 0],
                dst_ref=row_parts.at[turn, d],
                send_sem=row_send.at[turn, d],
                recv_sem=row_recv.at[turn, d],
                device_id=(peer[d], z),
                device_id_type=MESH,
            )
            copy.start()
            copies.append(copy)
        for copy in copies:
            copy.wait()
        total = part
        for d in range(1, shards):
            total = total + row_parts[turn, d].astype(jnp.float32)
        return total

    def col_exchange(turn, part):
        col_parts[turn, z] = part
        copies = []
        for k in range(1, replicas):
            copy = pltpu.make_async_remote_copy(
                src_ref=col_parts.at[turn, z],
                dst_ref=col_parts.at[turn, z],
                send_sem=col_send.at[turn, k],
                recv_sem=col_recv.at[turn, k],
                device_id=(me, zpeer[k]),
                device_id_type=MESH,
            )
            copy.start()
            copies.append(copy)
        for copy in copies:
            copy.wait()
        total = col_parts[turn, 0]
        for k in range(1, replicas):
            total = total + col_parts[turn, k]
        return total

    row_turn = 0
    col_turn = 0
    for loop_counter in range(ITERS):
        last = loop_counter == ITERS - 1
        for turn_index in range(SINK + 1):
            scaling = jnp.exp(duals_now)
            spread_scale(scaling)
            inverse = 1.0 / row_exchange(row_turn, row_pass())
            row_turn += 1
            if turn_index < SINK:
                mass = col_exchange(col_turn, col_pass(inverse) * scaling)
                col_turn += 1
                duals_now = duals_now + jnp.log(2.0 * target) - jnp.log(mass + target)

        dest = out_ref if last else cunit

        def raw_copy(i):
            rows = pl.ds(starts[i], group_rows[i])
            return pltpu.make_async_remote_copy(
                src_ref=raw_out.at[loop_counter, rows],
                dst_ref=raw_in.at[loop_counter, rows],
                send_sem=raw_send.at[loop_counter, i],
                recv_sem=raw_recv.at[loop_counter, i],
                device_id=(me, partner),
                device_id_type=MESH,
            )

        def pair_rows(i):
            return pl.ds(starts[i] // 2, group_rows[i] // 2)

        def pair_copy(i):
            return pltpu.make_async_remote_copy(
                src_ref=pair_out.at[loop_counter, pair_rows(i)],
                dst_ref=pair_in.at[loop_counter, pair_rows(i)],
                send_sem=pair_send.at[loop_counter, i],
                recv_sem=pair_recv.at[loop_counter, i],
                device_id=(me, middle),
                device_id_type=MESH,
            )

        def half_of(i, which):
            count = group_rows[i] // 2
            start = starts[i] + which * count
            if not isinstance(which, int):
                start = pl.multiple_of(start, 16)
            return pl.ds(start, count)

        def new_copy(i, which, to, number):
            return pltpu.make_async_remote_copy(
                src_ref=dest.at[half_of(i, which)],
                dst_ref=dest.at[half_of(i, which)],
                send_sem=new_send.at[loop_counter, i, number],
                recv_sem=new_recv.at[loop_counter, i, which],
                device_id=(me, to),
                device_id_type=MESH,
            )

        def new_arrive(i, which):
            ref = dest.at[half_of(i, which)]
            pltpu.make_async_copy(ref, ref, new_recv.at[loop_counter, i, which]).wait()

        own, other = z - 1, 2 - z

        def accumulate(j):
            rows = pl.ds(j * block, block)
            wide = jnp.concatenate([scale_cols[rows, :]] * tiles, axis=1)
            for p in range(shards):
                weights[:, slot_columns(p)] = (
                    inverse[p : p + 1, :] * kern[rows, slot_columns(p)] * wide
                ).astype(jnp.bfloat16)
            sums[rows, :] = jnp.dot(
                weights[...], units[...], preferred_element_type=jnp.float32
            )

            @pl.when(at_end)
            def _():
                raw_out[loop_counter, rows] = sums[rows, :].astype(jnp.bfloat16)
                for i in range(len(GROUP_PARTS)):
                    if j * block <= starts[i] < (j + 1) * block:
                        raw_copy(i).start()

        def pair_sums(i):
            @pl.when(in_mid)
            def _():
                raw_copy(i).wait_recv()
                rows = half_of(i, other)
                total = sums[rows, :] + raw_in[loop_counter, rows].astype(jnp.float32)
                pair_out[loop_counter, pair_rows(i)] = total.astype(jnp.bfloat16)
                pair_copy(i).start()

        def finish_sums(i):
            @pl.when(in_mid)
            def _():
                pair_copy(i).wait_recv()
                rows = half_of(i, own)
                total = sums[rows, :] + raw_in[loop_counter, rows].astype(jnp.float32)
                total = total + pair_in[loop_counter, pair_rows(i)].astype(jnp.float32)
                fresh = normalize(total)
                dest[rows, :] = fresh if last else normalize(fresh)
                new_copy(i, own, middle, 0).start()
                new_copy(i, own, partner, 1).start()

        def forward_new(i):
            @pl.when(in_mid)
            def _():
                new_arrive(i, other)
                new_copy(i, other, partner, 2).start()

        def end_new(i):
            @pl.when(at_end)
            def _():
                new_arrive(i, 0)
                new_arrive(i, 1)

        def remake(start, first, width):
            held = slice(first * point_rows, (first + width) * point_rows)
            scores = lax.dot_general(
                cunit[pl.ds(start, half_rows), :],
                units[held, :],
                (((1,), (1,)), ((), ())),
                preferred_element_type=jnp.float32,
            )
            for b in range(half_rows // span):
                line = start // span + b
                for p in range(width):
                    kern[pl.ds(start + b * span, span), slot_columns(first + p)] = (
                        jnp.exp(
                            scores[b * span : (b + 1) * span, slot_columns(p)] * inverse_soft
                        )
                        * masks[first + p, line : line + 1, :]
                    )

        count = len(GROUP_PARTS)
        early = [i for i in range(count) if starts[i] < half_rows]
        accumulate(0)
        accumulate(1)
        done = 2
        quarter = 0
        for step in range(count + 2):
            if step < count:
                pair_sums(step)
            if 0 <= step - 1 < count:
                finish_sums(step - 1)
            if 0 <= step - 2 < count:
                forward_new(step - 2)
            if done < SUM_BLOCKS:
                accumulate(done)
                done += 1
            if step - 2 >= len(early) - 1 and not last and quarter < 4:
                if quarter == 0:
                    for i in early:
                        end_new(i)
                remake(0, quarter * 2, 2)
                quarter += 1
        for i in range(count):
            if last or i not in early:
                end_new(i)
        if not last:
            remake(half_rows, 0, shards)
        for i in range(count):

            @pl.when(at_end)
            def _():
                raw_copy(i).wait_send()

            @pl.when(in_mid)
            def _():
                pair_copy(i).wait_send()
                new_copy(i, own, middle, 0).wait_send()
                new_copy(i, own, partner, 1).wait_send()
                new_copy(i, other, partner, 2).wait_send()

    duals_out_ref[...] = duals_now[:dual_rows]


def fused_body(points, centroids, owners, blocks, duals):
    point_rows, features = points.shape
    shard_rows = centroids.shape[0]
    shards = lax.axis_size("cent")
    replicas = lax.axis_size("rep")
    dims = (shards, replicas, point_rows, shard_rows, features)
    dual_rows = shard_rows // LANES
    dual_tile = duals.reshape(dual_rows, LANES)
    vmem = pl.BlockSpec(memory_space=pltpu.VMEM)
    row_turns = ITERS * (SINK + 1)
    col_turns = ITERS * SINK
    dma = pltpu.SemaphoreType.DMA
    count = len(GROUP_PARTS)
    new_centroids, duals_out = pl.pallas_call(
        functools.partial(fused_kernel, dims),
        out_shape=(
            jax.ShapeDtypeStruct((shard_rows, features), jnp.bfloat16),
            jax.ShapeDtypeStruct((dual_rows, LANES), jnp.float32),
        ),
        in_specs=[vmem] * 5,
        out_specs=(vmem, vmem),
        scratch_shapes=[
            pltpu.VMEM((shards * point_rows, features), jnp.bfloat16),
            pltpu.VMEM((shards, BLOCKS_DEV, point_rows), jnp.float32),
            pltpu.VMEM((shards, BLOCKS_DEV, point_rows), jnp.float32),
            pltpu.VMEM((shard_rows, shards * point_rows), jnp.float32),
            pltpu.VMEM((shard_rows, features), jnp.bfloat16),
            pltpu.VMEM((shard_rows, LANES), jnp.float32),
            pltpu.VMEM((shard_rows, LANES), jnp.float32),
            pltpu.VMEM((shard_rows // SUM_BLOCKS, shards * point_rows), jnp.bfloat16),
            pltpu.VMEM((shard_rows, features), jnp.float32),
            pltpu.VMEM((row_turns, shards, shards, point_rows), jnp.bfloat16),
            pltpu.VMEM((col_turns, replicas, SUBLANES, LANES), jnp.float32),
            pltpu.VMEM((ITERS, shard_rows, features), jnp.bfloat16),
            pltpu.VMEM((ITERS, shard_rows, features), jnp.bfloat16),
            pltpu.VMEM((ITERS, shard_rows // 2, features), jnp.bfloat16),
            pltpu.VMEM((ITERS, shard_rows // 2, features), jnp.bfloat16),
            dma((shards, 4, 3)),
            dma((shards, 4)),
            dma((shards,)),
            dma((shards,)),
            dma((row_turns, shards)),
            dma((row_turns, shards)),
            dma((col_turns, replicas)),
            dma((col_turns, replicas)),
            dma((ITERS, count)),
            dma((ITERS, count)),
            dma((ITERS, count)),
            dma((ITERS, count)),
            dma((ITERS, count, 3)),
            dma((ITERS, count, 2)),
        ],
        compiler_params=pltpu.CompilerParams(
            collective_id=0, has_side_effects=True, vmem_limit_bytes=VMEM_LIMIT
        ),
        name="fused_kmeans",
    )(points, centroids, owners.T, jnp.transpose(blocks, (1, 2, 0)), dual_tile)
    return new_centroids, duals_out.reshape(shard_rows)


def solution(mesh):
    shards = mesh.shape["cent"]

    def body(points, centroids, owners, blocks, duals):
        point_rows, features = points.shape
        shard_rows = centroids.shape[0]
        plane_bytes = shards * point_rows * (2 * features + 4 * shard_rows)
        cube = shards == 2**3 and mesh.shape["rep"] == 2 * 2 and shard_rows % (2 * SUBLANES * 2 * sum(GROUP_PARTS)) == 0 and SUBLANES % (shard_rows // LANES) == 0
        if cube and plane_bytes <= VMEM_LIMIT // 3:
            return fused_body(points, centroids, owners, blocks, duals)
        return routed_body(points, centroids, owners, blocks, duals)

    return jax.shard_map(
        body,
        mesh=mesh,
        in_specs=(
            P(("cent", "rep"), None),
            P("cent", None),
            P(("cent", "rep"), None),
            P(("cent", "rep"), None, None),
            P("cent"),
        ),
        out_specs=(P("cent", None), P("cent")),
        check_vma=False,
    )
```

time: 203 us -> 195 us (0.961)
  Pallas kernels: 198 us -> 191 us
    pallas_call x1, Pallas kernels: 198 us -> 191 us  [fused_body(): pl.pallas_call(functools.partial(fused_kernel, dims), out_shape=(jax.Shap...]
where the time goes in v1:
time: 195 us
  Pallas kernels  191 us (98%)
  local copies, waits for them, and re-layouts  2.85 us (1%)
    pallas_call x1, Pallas kernels, fused_body(): pl.pallas_call(functools.partial(fused_kernel, dims), out_shape=(jax.Shap...  191 us

profile of v1, /device:TPU:0, one launch (start us, length us, event | category | flops | bytes accessed | tf_op | source)
XLA Modules:
  0.0 194.8 jit_solution(15798813046494208825)
XLA Ops:
  0.6 191.3 %fused_kmeans.1 = (bf16[512,1024]{1,0:T(8,128)(2,1)}, f32[4,128]{1,0:T(4,128)}) custom-call(bf16[512,1024]{1,0:T(8,128)(2,1)} %points_ref.1, bf16[512,1024]{1,0:T(8,128)(2,1)} %centroids_ref.1, s32[2,512]{1,0:T(2,128)} %bitcast.5, s32[2,4,512]{2,1,0:T(4,128)} %bitcast.4, f32[4,128]{1,0:T(4,128)} %bitcast.6), custom_call_target="tpu_custom_call" | custom-call | tf_op jit(solution)/shard_map/fused_kmeans/pallas_call | solution.py:603
  191.9 0.0 copy-start
  191.9 2.3 %copy.9 = bf16[512,1024]{1,0:T(8,128)(2,1)} copy(bf16[512,1024]{1,0:T(8,128)(2,1)} %get-tuple-element.8) | data formatting | bytes 2097152
  194.2 0.0 copy-done
  194.2 0.6 copy.10
Async XLA Ops:
  191.9 2.3 %copy-start = (f32[4,128]{1,0:T(4,128)S(1)}, f32[4,128]{1,0:T(4,128)}, u32[]{:S(2)}) copy-start(f32[4,128]{1,0:T(4,128)} %get-tuple-element.5) | copy-start | bytes 6148

commit v2 on v1

--- a/solution.py
+++ b/solution.py
@@ -14,7 +14,8 @@
 LANES = 128
 SUBLANES = 8
 SUM_BLOCKS = 4
-GROUP_PARTS = (1, 1, 2, 2, 2, 2, 2, 2, 1, 1)
+GROUP_PARTS = (2,) * 8
+DELIVER = 2
 MESH = pl.DeviceIdType.MESH
 VMEM_LIMIT = 64000000
 
@@ -132,6 +133,7 @@
     cunit,
     scale_cols,
     mass_cols,
+    first_parts,
     weights,
     sums,
     row_parts,
@@ -154,6 +156,7 @@
     pair_recv,
     new_send,
     new_recv,
+    fetch,
 ):
     shards, replicas, point_rows, shard_rows, features = dims
     span = shard_rows // BLOCKS_DEV
@@ -199,8 +202,11 @@
         start = peer[slot] * point_rows + chunk * piece
         return pl.ds(pl.multiple_of(start, piece), piece * count)
 
-    for step in (0, 2, 1, 3):
-        units[chunk_rows(0, step), :] = normalize(points_ref[pl.ds(step * piece, piece), :])
+    held_points = units.at[chunk_rows(0, 0, pieces)]
+    point_copy = pltpu.make_async_copy(points_ref, held_points, fetch.at[0])
+    point_copy.start()
+    centroid_copy = pltpu.make_async_copy(centroids_ref, cunit, fetch.at[1])
+    centroid_copy.start()
 
     number = lax.broadcasted_iota(jnp.int32, (BLOCKS_DEV, point_rows), 0)
     named = []
@@ -214,6 +220,10 @@
         for r in range(1, routes):
             marked = jnp.logical_or(marked, jnp.logical_and(owners_ref[r : r + 1, :] == s, named[r]))
         marks_out[s] = jnp.where(marked, 1.0, 0.0)
+
+    point_copy.wait()
+    for step in (0, 2, 1, 3):
+        units[chunk_rows(0, step), :] = normalize(units[chunk_rows(0, step), :])
 
     pl.semaphore_wait(barrier, shards - 1 + replicas - 1)
 
@@ -262,7 +272,23 @@
         push(0, step, 1)
     masks[me] = marks_out[me]
 
-    cunit[...] = normalize(centroids_ref[...])
+    centroid_copy.wait()
+    cunit[...] = normalize(cunit[...])
+
+    duals_now = jnp.concatenate([duals_ref[...]] * (SUBLANES // dual_rows), axis=0)
+
+    def spread_scale(scaling):
+        for t in range(dual_rows):
+            row = jnp.broadcast_to(scaling[t : t + 1, :], (LANES, LANES))
+            scale_cols[pl.ds(t * LANES, LANES), :] = row.T
+
+    spread_scale(jnp.exp(duals_now))
+
+    def fold(values, start):
+        width = values.shape[1]
+        wide = jnp.concatenate([scale_cols[pl.ds(start, span), :]] * (width // LANES), axis=1)
+        scaled = (values * wide).reshape(span // SUBLANES, SUBLANES, width)
+        return jnp.sum(scaled, axis=0)
 
     def block_kernel(slot, chunk, count):
         held = chunk_rows(slot, chunk, count)
@@ -273,10 +299,12 @@
             preferred_element_type=jnp.float32,
         )
         marks = masks[peer[slot], :, pl.ds(chunk * piece, count * piece)]
+        part = jnp.zeros((SUBLANES, count * piece), jnp.float32)
         for b in range(BLOCKS_DEV):
-            kern[pl.ds(b * span, span), held] = (
-                jnp.exp(scores[b * span : (b + 1) * span] * inverse_soft) * marks[b : b + 1, :]
-            )
+            values = jnp.exp(scores[b * span : (b + 1) * span] * inverse_soft) * marks[b : b + 1, :]
+            kern[pl.ds(b * span, span), held] = values
+            part = part + fold(values, b * span)
+        first_parts[peer[slot], :, pl.ds(chunk * piece, count * piece)] = part
 
     def half_kernels(halves):
         for slot, chunks in halves:
@@ -325,17 +353,11 @@
     for copy in mask_copies:
         copy.wait_send()
 
-    duals_now = jnp.concatenate([duals_ref[...]] * (SUBLANES // dual_rows), axis=0)
     groups = shard_rows // SUBLANES
     tiles = point_rows // LANES
 
     def slot_columns(p):
         return slice(p * point_rows, (p + 1) * point_rows)
-
-    def spread_scale(scaling):
-        for t in range(dual_rows):
-            row = jnp.broadcast_to(scaling[t : t + 1, :], (LANES, LANES))
-            scale_cols[pl.ds(t * LANES, LANES), :] = row.T
 
     def row_pass():
         def step(g, acc):
@@ -418,8 +440,14 @@
         last = loop_counter == ITERS - 1
         for turn_index in range(SINK + 1):
             scaling = jnp.exp(duals_now)
-            spread_scale(scaling)
-            inverse = 1.0 / row_exchange(row_turn, row_pass())
+            if turn_index == 0:
+                part = jnp.concatenate(
+                    [jnp.sum(first_parts[p], axis=0, keepdims=True) for p in range(shards)], axis=0
+                )
+            else:
+                spread_scale(scaling)
+                part = row_pass()
+            inverse = 1.0 / row_exchange(row_turn, part)
             row_turn += 1
             if turn_index < SINK:
                 mass = col_exchange(col_turn, col_pass(inverse) * scaling)
@@ -534,15 +562,20 @@
                 (((1,), (1,)), ((), ())),
                 preferred_element_type=jnp.float32,
             )
-            for b in range(half_rows // span):
-                line = start // span + b
-                for p in range(width):
-                    kern[pl.ds(start + b * span, span), slot_columns(first + p)] = (
-                        jnp.exp(
-                            scores[b * span : (b + 1) * span, slot_columns(p)] * inverse_soft
-                        )
+            for p in range(width):
+                if start == 0:
+                    part = jnp.zeros((SUBLANES, point_rows), jnp.float32)
+                else:
+                    part = first_parts[first + p]
+                for b in range(half_rows // span):
+                    line = start // span + b
+                    values = (
+                        jnp.exp(scores[b * span : (b + 1) * span, slot_columns(p)] * inverse_soft)
                         * masks[first + p, line : line + 1, :]
                     )
+                    kern[pl.ds(start + b * span, span), slot_columns(first + p)] = values
+                    part = part + fold(values, start + b * span)
+                first_parts[first + p] = part
 
         count = len(GROUP_PARTS)
         early = [i for i in range(count) if starts[i] < half_rows]
@@ -596,6 +629,7 @@
     dual_rows = shard_rows // LANES
     dual_tile = duals.reshape(dual_rows, LANES)
     vmem = pl.BlockSpec(memory_space=pltpu.VMEM)
+    hbm = pl.BlockSpec(memory_space=pltpu.HBM)
     row_turns = ITERS * (SINK + 1)
     col_turns = ITERS * SINK
     dma = pltpu.SemaphoreType.DMA
@@ -606,7 +640,7 @@
             jax.ShapeDtypeStruct((shard_rows, features), jnp.bfloat16),
             jax.ShapeDtypeStruct((dual_rows, LANES), jnp.float32),
         ),
-        in_specs=[vmem] * 5,
+        in_specs=[hbm, hbm, vmem, vmem, vmem],
         out_specs=(vmem, vmem),
         scratch_shapes=[
             pltpu.VMEM((shards * point_rows, features), jnp.bfloat16),
@@ -616,6 +650,7 @@
             pltpu.VMEM((shard_rows, features), jnp.bfloat16),
             pltpu.VMEM((shard_rows, LANES), jnp.float32),
             pltpu.VMEM((shard_rows, LANES), jnp.float32),
+            pltpu.VMEM((shards, SUBLANES, point_rows), jnp.float32),
             pltpu.VMEM((shard_rows // SUM_BLOCKS, shards * point_rows), jnp.bfloat16),
             pltpu.VMEM((shard_rows, features), jnp.float32),
             pltpu.VMEM((row_turns, shards, shards, point_rows), jnp.bfloat16),
@@ -638,13 +673,37 @@
             dma((ITERS, count)),
             dma((ITERS, count, 3)),
             dma((ITERS, count, 2)),
+            dma((2,)),
         ],
         compiler_params=pltpu.CompilerParams(
             collective_id=0, has_side_effects=True, vmem_limit_bytes=VMEM_LIMIT
         ),
         name="fused_kmeans",
     )(points, centroids, owners.T, jnp.transpose(blocks, (1, 2, 0)), dual_tile)
+    new_centroids, duals_out = deliver(new_centroids, duals_out)
     return new_centroids, duals_out.reshape(shard_rows)
+
+
+def deliver_kernel(rows_ref, line_ref, rows_out_ref, line_out_ref):
+    rows_out_ref[...] = rows_ref[...]
+    line_out_ref[...] = line_ref[...]
+
+
+def deliver(rows, line):
+    count, features = rows.shape
+    tile = pl.BlockSpec((count // DELIVER, features), lambda i: (i, 0))
+    whole = pl.BlockSpec(line.shape, lambda i: (0, 0))
+    return pl.pallas_call(
+        deliver_kernel,
+        grid=(DELIVER,),
+        out_shape=(
+            jax.ShapeDtypeStruct(rows.shape, rows.dtype),
+            jax.ShapeDtypeStruct(line.shape, line.dtype),
+        ),
+        in_specs=[tile, whole],
+        out_specs=(tile, whole),
+        name="deliver",
+    )(rows, line)
 
 
 def solution(mesh):

time: 195 us -> 189 us (0.969)
  Pallas kernels: 191 us -> 188 us
  local copies, waits for them, and re-layouts: 2.85 us -> 0 us
    pallas_call x1, Pallas kernels: 191 us -> 186 us  [fused_body(): pl.pallas_call(functools.partial(fused_kernel, dims), out_shape=(jax.Shap...]
    unnamed x4 -> x0, local copies, waits for them, and re-layouts: 2.85 us -> none
    pallas_call x0 -> x1, Pallas kernels: none -> 2.06 us  [deliver(): pl.pallas_call(deliver_kernel, grid=(DELIVER,), out_shape=(jax.ShapeDtype...]
where the time goes in v2:
time: 189 us; the launch traced here: 188 us
  Pallas kernels  188 us (99%)
    pallas_call x1, Pallas kernels, fused_body(): pl.pallas_call(functools.partial(fused_kernel, dims), out_shape=(jax.Shap...  186 us

profile of v2, /device:TPU:0, one launch (start us, length us, event | category | flops | bytes accessed | tf_op | source)
XLA Modules:
  0.0 188.3 jit_solution(5454543239121230585)
XLA Ops:
  0.6 185.6 %fused_kmeans.1 = (bf16[512,1024]{1,0:T(8,128)(2,1)}, f32[4,128]{1,0:T(4,128)}) custom-call(bf16[512,1024]{1,0:T(8,128)(2,1)} %points_ref.1, bf16[512,1024]{1,0:T(8,128)(2,1)} %centroids_ref.1, s32[2,512]{1,0:T(2,128)} %bitcast.5, s32[2,4,512]{2,1,0:T(4,128)} %bitcast.4, f32[4,128]{1,0:T(4,128)} %bitcast.6), custom_call_target="tpu_custom_call" | custom-call | tf_op jit(solution)/shard_map/fused_kmeans/pallas_call | solution.py:637
  186.3 2.1 %deliver.1 = (bf16[512,1024]{1,0:T(8,128)(2,1)}, f32[4,128]{1,0:T(4,128)}) custom-call(bf16[512,1024]{1,0:T(8,128)(2,1)} %get-tuple-element.6.rows_ref, f32[4,128]{1,0:T(4,128)} %get-tuple-element.7.line_ref), custom_call_target="tpu_custom_call" | custom-call | tf_op jit(solution)/shard_map/deliver/pallas_call | solution.py:696

commit v3 on v2

--- a/solution.py
+++ b/solution.py
@@ -581,7 +581,8 @@
         early = [i for i in range(count) if starts[i] < half_rows]
         accumulate(0)
         accumulate(1)
-        done = 2
+        accumulate(2)
+        done = 3
         quarter = 0
         for step in range(count + 2):
             if step < count:

time: 189 us -> 189 us (level)
  no operation moved by 1% of the time
where the time goes in v3:
time: 189 us; the launch traced here: 188 us
  Pallas kernels  188 us (99%)
    pallas_call x1, Pallas kernels, fused_body(): pl.pallas_call(functools.partial(fused_kernel, dims), out_shape=(jax.Shap...  186 us

profile of v3, /device:TPU:0, one launch (start us, length us, event | category | flops | bytes accessed | tf_op | source)
XLA Modules:
  0.0 188.3 jit_solution(12327234811657520393)
XLA Ops:
  0.6 185.6 %fused_kmeans.1 = (bf16[512,1024]{1,0:T(8,128)(2,1)}, f32[4,128]{1,0:T(4,128)}) custom-call(bf16[512,1024]{1,0:T(8,128)(2,1)} %points_ref.1, bf16[512,1024]{1,0:T(8,128)(2,1)} %centroids_ref.1, s32[2,512]{1,0:T(2,128)} %bitcast.5, s32[2,4,512]{2,1,0:T(4,128)} %bitcast.4, f32[4,128]{1,0:T(4,128)} %bitcast.6), custom_call_target="tpu_custom_call" | custom-call | tf_op jit(solution)/shard_map/fused_kmeans/pallas_call | solution.py:638
  186.3 2.1 %deliver.1 = (bf16[512,1024]{1,0:T(8,128)(2,1)}, f32[4,128]{1,0:T(4,128)}) custom-call(bf16[512,1024]{1,0:T(8,128)(2,1)} %get-tuple-element.6.rows_ref, f32[4,128]{1,0:T(4,128)} %get-tuple-element.7.line_ref), custom_call_target="tpu_custom_call" | custom-call | tf_op jit(solution)/shard_map/deliver/pallas_call | solution.py:697
